TPU v7x, 32 devices: a whole 2x2x4 slice. The times are simulated.
32 devices in a mesh: groups: 2 (over x), row: 8 (over z, y), col: 2 (over core).
Axes of the slice: x: 2, y: 2, z: 4, core: 2. Of those that a mesh axis runs over, the one named last changes fastest.
Arguments:
- queries: bfloat16 [8192, 1024], P(('groups', 'row', 'col')), parts along dimension 0, may hold values from -200 to 200
- keys: bfloat16 [8192, 128], P(('groups', 'row', 'col')), parts along dimension 0, may hold values from -5 to 5
- values: bfloat16 [8192, 128], P(('groups', 'row', 'col')), parts along dimension 0, may hold values from -6 to 6
- doc_lengths: int32 [32], P('groups'), parts along dimension 0, may hold values from 1 to 3072, 4096 in all
Outputs:
- attended: bfloat16 [8192, 1024], P(('groups', 'row', 'col')), parts along dimension 0
There are 2 independent parts, one for each index of `groups`. A program takes and returns all parts, laid end to end along the dimension named above; each array names one. Nothing has to cross between parts.
Inputs may be any that keep to these rules, and one draw needn't show every extreme that they name: `doc_lengths`: the 16 lengths sum to 4096 and the longest is exactly 3072.
All inputs are finite; a program needn't handle non-finite values.
Results may differ from a plain program's by a relative error of at most 0.0055.
Values may be sent and summed in bfloat16 or wider, within the bound.
A program may use at most 64 MiB of HBM per device.

v0:
```python
import functools

import jax
import jax.numpy as jnp
from jax import lax
from jax.experimental import pallas as pl
from jax.experimental.pallas import tpu as pltpu
from jax.sharding import PartitionSpec as P

HEAD_DIM = 128
RATE = HEAD_DIM ** (-0.5) * 1.4426950408889634
MASKED = -1e30
AHEAD_SLOTS = 8


def kernel(
    n_row,
    n_col,
    lanes,
    reach,
    lens_ref,
    q_ref,
    k_ref,
    v_ref,
    o_ref,
    kbuf,
    vbuf,
    top_ref,
    total_ref,
    acc_ref,
    qa_ref,
    s_ref,
    load_sem,
    in_sem,
    mate_sem,
    up_send,
    cross_send,
    mate_send,
):
    shard = q_ref.shape[0]
    heads = q_ref.shape[1] // HEAD_DIM
    levels = n_row // lanes
    steps = 2 * (min(levels - 1, (reach + lanes - 1) // lanes) + 1)
    row = lax.axis_index("row")
    col = lax.axis_index("col")
    level = row // lanes
    lane = row % lanes
    mate = 1 - col
    other = level * lanes + (lanes - 1 - lane)
    mine = pl.ds(pl.multiple_of(col * shard, shard), shard)
    theirs = pl.ds(pl.multiple_of(mate * shard, shard), shard)

    def needs(reader, source):
        return (source >= 0) & (reader > source) & (reader - source <= reach)

    has_up = level + 1 < levels
    has_down = level > 0
    has_other = lanes > 1

    barrier = pltpu.get_barrier_semaphore()
    pl.semaphore_signal(barrier, inc=1, device_id={"col": mate})
    if has_other:
        pl.semaphore_signal(barrier, inc=1, device_id={"row": other})

    @pl.when(has_up)
    def _():
        pl.semaphore_signal(barrier, inc=1, device_id={"row": row + lanes})

    @pl.when(has_down)
    def _():
        pl.semaphore_signal(barrier, inc=1, device_id={"row": row - lanes})

    loads = [
        pltpu.make_async_copy(k_ref, kbuf.at[row, mine, :], load_sem.at[0]),
        pltpu.make_async_copy(v_ref, vbuf.at[row, mine, :], load_sem.at[1]),
    ]
    for head in range(heads):
        part = q_ref.at[:, head * HEAD_DIM : (head + 1) * HEAD_DIM]
        loads.append(
            pltpu.make_async_copy(part, qa_ref.at[head, :, :HEAD_DIM], load_sem.at[2 + head])
        )
    for load in loads:
        load.start()

    count = 1 + int(has_other) + has_up.astype(jnp.int32) + has_down.astype(jnp.int32)
    pl.semaphore_wait(barrier, count)

    def send(src, buf, source, which, j, sends, recvs, at, device):
        return pltpu.make_async_remote_copy(
            src_ref=src,
            dst_ref=buf.at[source, mine, :],
            send_sem=sends.at[which, j],
            recv_sem=recvs.at[which, at],
            device_id=device,
            device_id_type=pl.DeviceIdType.MESH,
        )

    def source_of(j):
        dist, kind = j // 2, j % 2
        cross = kind == 1
        from_lane = jnp.where(cross, lanes - 1 - lane, lane)
        source = (level - dist) * lanes + from_lane
        if lanes == 1:
            source = jnp.where(cross, -1, source)
        return source

    def relays(j, source, straight):
        mate_wants = (source < row) | (col < mate)
        found = [(mate_wants, mate_send, mate_sem, j, {"col": mate})]
        up = straight & has_up & needs(row + lanes, source)
        found.append((up, up_send, in_sem, j + 2, {"row": row + lanes}))
        if has_other:
            cross = straight & needs(other, source)
            found.append((cross, cross_send, in_sem, j + 1, {"row": other}))
        return found

    def forward(src, buf, source, which, j, straight):
        for wanted, sends, recvs, at, device in reversed(relays(j, source, straight)):

            @pl.when(wanted)
            def _():
                send(src, buf, source, which, j, sends, recvs, at, device).start()

    def arrived(buf, source, which, j, sems, part):
        here = buf.at[source, part, :]
        pltpu.make_async_copy(here, here, sems.at[which, j]).wait()

    forward(k_ref, kbuf, row, 0, 0, True)
    forward(v_ref, vbuf, row, 1, 0, True)

    first = (row * n_col + col) * shard
    qpos = first + lax.broadcasted_iota(jnp.int32, (1, shard), 1)

    def within(places):
        return (places >= begins) & (places < ends)

    lanes_of = lax.broadcasted_iota(jnp.int32, (1, HEAD_DIM), 1)
    begins = jnp.zeros((1, HEAD_DIM), jnp.int32)
    ends = jnp.full((1, HEAD_DIM), n_row * n_col * shard, jnp.int32)
    end = jnp.int32(0)
    docs = lens_ref.shape[0]
    for doc in range(docs):
        begins = jnp.where(lanes_of == doc, end, begins)
        end = end + lens_ref[doc]
        ends = jnp.where(lanes_of == doc, end, ends)
    qplace = first + lax.broadcasted_iota(jnp.int32, (shard, HEAD_DIM), 0)
    member = jnp.where(within(qplace) & (lanes_of < docs), 1.0, 0.0).astype(jnp.bfloat16)
    for head in range(heads):
        qa_ref[head, :, HEAD_DIM:] = member
    for load in loads:
        load.wait()

    def attend(kblock, vblock, kfirst, fresh):
        count = kblock.shape[0]
        kplace = kfirst + lax.broadcasted_iota(jnp.int32, (count, HEAD_DIM), 0)
        apart = jnp.where(within(kplace), 0.0, MASKED).astype(jnp.bfloat16)
        kwide = jnp.concatenate([kblock, apart], axis=1)
        if fresh:
            kpos = kfirst + lax.broadcasted_iota(jnp.int32, (count, shard), 0)
            bias = jnp.where(kpos <= qpos, jnp.float32(0.0), jnp.float32(MASKED))
        vflip = vblock.T

        def score(head):
            scores = lax.dot_general(
                kwide, qa_ref[head], (((1,), (1,)), ((), ())), preferred_element_type=jnp.float32
            )
            if fresh:
                scores = scores + bias
            s_ref[head % AHEAD_SLOTS, :count, :] = scores
            top = jnp.max(scores, axis=0, keepdims=True)
            if fresh:
                return top, top
            before = top_ref[head : head + 1, :]
            return before, jnp.maximum(before, top)

        tops = [score(head) for head in range(AHEAD_SLOTS - 1)]
        for head in range(heads):
            before, top = tops[head]
            if head + AHEAD_SLOTS - 1 < heads:
                tops.append(score(head + AHEAD_SLOTS - 1))
            weights = jnp.exp2((s_ref[head % AHEAD_SLOTS, :count, :] - top) * RATE)
            total = jnp.sum(weights, axis=0, keepdims=True)
            summed = jnp.dot(
                vflip, weights.astype(jnp.bfloat16), preferred_element_type=jnp.float32
            )
            if not fresh:
                factor = jnp.exp2((before - top) * RATE)
                total = total + total_ref[head : head + 1, :] * factor
                summed = summed + acc_ref[head] * factor
            top_ref[head : head + 1, :] = top
            total_ref[head : head + 1, :] = total
            acc_ref[head] = summed

    attend(kbuf[row, mine, :], vbuf[row, mine, :], first, True)

    def relay(j, least):
        source = source_of(j)

        @pl.when((j >= least) & (j < steps) & needs(row, source))
        def _():
            for which, buf in enumerate((kbuf, vbuf)):
                arrived(buf, source, which, j, in_sem, mine)
                forward(buf.at[source, mine, :], buf, source, which, j, j % 2 == 0)

    relay(jnp.int32(2), 1)
    relay(jnp.int32(1), 1)

    @pl.when(col > 0)
    def _():
        arrived(kbuf, row, 0, 0, mate_sem, theirs)
        arrived(vbuf, row, 1, 0, mate_sem, theirs)
        attend(kbuf[row, :shard, :], vbuf[row, :shard, :], row * n_col * shard, False)

    @pl.loop(1, steps)
    def _(j):
        source = source_of(j)

        @pl.when(needs(row, source))
        def _():
            arrived(kbuf, source, 0, j, mate_sem, theirs)
            arrived(vbuf, source, 1, j, mate_sem, theirs)
            attend(kbuf[source], vbuf[source], source * n_col * shard, False)

        ahead = 2 * (j - jnp.where(lane == lanes - 1, 0, 1)) + 1
        relay(ahead + 1, 3)
        relay(ahead, 3)

    for head in range(heads):
        inverse = 1.0 / total_ref[head : head + 1, :]
        result = (acc_ref[head] * inverse).T
        o_ref[:, head * HEAD_DIM : (head + 1) * HEAD_DIM] = result.astype(o_ref.dtype)

    @pl.loop(0, steps)
    def _(j):
        source = source_of(j)

        @pl.when(needs(row, source) | (j == 0))
        def _():
            for wanted, sends, recvs, at, device in relays(j, source, j % 2 == 0):

                @pl.when(wanted)
                def _():
                    for which, buf in enumerate((kbuf, vbuf)):
                        part = buf.at[source, mine, :]
                        send(part, buf, source, which, j, sends, recvs, at, device).wait_send()


def shards(n_row, n_col, queries, keys, values, doc_lengths):
    shard, width = queries.shape
    lanes = 2 if n_row % 2 == 0 else 1
    span = shard * n_row * n_col
    longest = (3 * span) // 4
    reach = min(n_row - 1, -(-longest // (shard * n_col)))
    levels = n_row // lanes
    steps = 2 * (min(levels - 1, (reach + lanes - 1) // lanes) + 1)
    tile = shard * n_col
    heads = width // HEAD_DIM
    vmem = pl.BlockSpec(memory_space=pltpu.VMEM)
    whole = pl.BlockSpec(memory_space=pltpu.HBM)
    sems = pltpu.SemaphoreType.DMA((2, steps))
    return pl.pallas_call(
        functools.partial(kernel, n_row, n_col, lanes, reach),
        out_shape=jax.ShapeDtypeStruct(queries.shape, queries.dtype),
        in_specs=[pl.BlockSpec(memory_space=pltpu.SMEM), whole, whole, whole],
        out_specs=vmem,
        scratch_shapes=[
            pltpu.VMEM((n_row, tile, HEAD_DIM), keys.dtype),
            pltpu.VMEM((n_row, tile, HEAD_DIM), values.dtype),
            pltpu.VMEM((heads, shard), jnp.float32),
            pltpu.VMEM((heads, shard), jnp.float32),
            pltpu.VMEM((heads, HEAD_DIM, shard), jnp.float32),
            pltpu.VMEM((heads, shard, 2 * HEAD_DIM), queries.dtype),
            pltpu.VMEM((AHEAD_SLOTS, tile, shard), jnp.float32),
            pltpu.SemaphoreType.DMA((2 + heads,)),
            sems,
            sems,
            sems,
            sems,
            sems,
        ],
        compiler_params=pltpu.CompilerParams(
            collective_id=0, has_side_effects=True, vmem_limit_bytes=24 << 20
        ),
        name="attend",
    )(*(pltpu.with_memory_space_constraint(x, pltpu.HBM) for x in (doc_lengths, queries, keys, values)))


def solution(mesh):
    placed = P(("groups", "row", "col"), None)
    return jax.shard_map(
        functools.partial(shards, mesh.shape["row"], mesh.shape["col"]),
        mesh=mesh,
        in_specs=(placed, placed, placed, P("groups")),
        out_specs=placed,
        check_vma=False,
    )
```

profile of v0, /device:TPU:25, one launch (start us, length us, event | category | flops | bytes accessed | tf_op | source)
XLA Modules:
  0.0 24.0 jit_solution(10878728420717347482)
XLA Ops:
  0.0 23.2 %attend.1 = bf16[256,1024]{1,0:T(8,128)(2,1)S(1)} custom-call(s32[16]{0:T(128)} %lens_ref.1, bf16[256,1024]{1,0:T(8,128)(2,1)} %q_ref.1, bf16[256,128]{1,0:T(8,128)(2,1)} %k_ref.1, bf16[256,128]{1,0:T(8,128)(2,1)} %v_ref.1), custom_call_target="tpu_custom_call" | custom-call | tf_op jit(solution)/shard_map/attend/pallas_call | solution.py:261
  23.2 0.8 %copy.6 = bf16[256,1024]{1,0:T(8,128)(2,1)} copy(bf16[256,1024]{1,0:T(8,128)(2,1)S(1)} %attend.1) | data formatting | bytes 1048576
where the time goes:
time: 24.1 us; the launch traced here: 24 us
  Pallas kernels  23.2 us (96%)
  local copies, waits for them, and re-layouts  0.8 us (3%)
    pallas_call x1, Pallas kernels, shards(): pl.pallas_call(functools.partial(kernel, n_row, n_col, lanes, reach), out...  23.2 us
    unnamed x1, local copies, waits for them, and re-layouts  0.8 us

commit v1 on v0

v1 whole, which is shorter than its diff:
```python
import functools

import jax
import jax.numpy as jnp
from jax import lax
from jax.experimental import pallas as pl
from jax.experimental.pallas import tpu as pltpu
from jax.sharding import PartitionSpec as P

HEAD_DIM = 128
RATE = HEAD_DIM ** (-0.5) * 1.4426950408889634
MASKED = -1e30
AHEAD_SLOTS = 8
SUM_ROWS = 16
PIECES = 2


def kernel(
    n_row,
    n_col,
    lanes,
    reach,
    lens_ref,
    q_hbm,
    k_hbm,
    v_hbm,
    o_ref,
    kv,
    q_ref,
    member_ref,
    top_ref,
    total_ref,
    acc_ref,
    s_ref,
    load_sem,
    in_sem,
    mate_sem,
    up_send,
    cross_send,
    mate_send,
):
    shard = q_hbm.shape[0]
    heads = q_hbm.shape[1] // HEAD_DIM
    levels = n_row // lanes
    tile = n_col * shard
    piece = 2 * shard // PIECES
    furthest = min(levels - 1, (reach + lanes - 1) // lanes)
    has_other = lanes > 1
    row = lax.axis_index("row")
    col = lax.axis_index("col")
    level = row // lanes
    lane = row % lanes
    mate = 1 - col
    other = level * lanes + (lanes - 1 - lane)
    has_up = level + 1 < levels
    has_down = level > 0

    def needs(reader, source):
        return (source >= 0) & (reader > source) & (reader - source <= reach)

    def straight(dist):
        return row - dist * lanes

    def crossed(dist):
        return other - dist * lanes

    barrier = pltpu.get_barrier_semaphore()
    pl.semaphore_signal(barrier, inc=1, device_id={"col": mate})
    if has_other:
        pl.semaphore_signal(barrier, inc=1, device_id={"row": other})

    @pl.when(has_up)
    def _():
        pl.semaphore_signal(barrier, inc=1, device_id={"row": row + lanes})

    @pl.when(has_down)
    def _():
        pl.semaphore_signal(barrier, inc=1, device_id={"row": row - lanes})

    load_k = pltpu.make_async_copy(k_hbm, kv.at[row, col, :shard, :], load_sem.at[0])
    load_v = pltpu.make_async_copy(v_hbm, kv.at[row, col, shard:, :], load_sem.at[1])
    load_q = pltpu.make_async_copy(q_hbm, q_ref, load_sem.at[2])
    for load in (load_k, load_v, load_q):
        load.start()

    def copy(source, rows, send_sem, recv_sem, device):
        here = kv.at[source, col, rows, :]
        return pltpu.make_async_remote_copy(
            src_ref=here,
            dst_ref=here,
            send_sem=send_sem,
            recv_sem=recv_sem,
            device_id=device,
            device_id_type=pl.DeviceIdType.MESH,
        )

    def part(p):
        return pl.ds(p * piece, piece)

    def to_up(source, p, dist):
        recv = in_sem.at[2 * dist + 2, p]
        return copy(source, part(p), up_send.at[dist], recv, {"row": row + lanes})

    def to_other(source, p, dist):
        recv = in_sem.at[2 * dist + 1, p]
        return copy(source, part(p), cross_send.at[dist], recv, {"row": other})

    def to_mate(source, unit):
        whole = pl.ds(0, 2 * shard)
        return copy(source, whole, mate_send.at[unit], mate_sem.at[unit], {"col": mate})

    def wait_whole(source, sem):
        here = kv.at[source, col, :, :]
        pltpu.make_async_copy(here, here, sem).wait()

    def wait_part(source, p, sem):
        here = kv.at[source, col, part(p), :]
        pltpu.make_async_copy(here, here, sem).wait()

    own_up = has_up
    own_cross = needs(other, row)
    own_mate = col < mate

    count = 1 + int(has_other) + has_up.astype(jnp.int32) + has_down.astype(jnp.int32)
    pl.semaphore_wait(barrier, count)
    load_k.wait()
    load_v.wait()

    @pl.when(own_up)
    def _():
        for p in range(PIECES):
            to_up(row, p, 0).start()

    if has_other:

        @pl.when(own_cross)
        def _():
            for p in range(PIECES):
                to_other(row, p, 0).start()

    @pl.when(own_mate)
    def _():
        to_mate(row, 0).start()

    first = (row * n_col + col) * shard
    qpos = first + lax.broadcasted_iota(jnp.int32, (1, shard), 1)

    def within(places):
        return (places >= begins) & (places < ends)

    lanes_of = lax.broadcasted_iota(jnp.int32, (1, HEAD_DIM), 1)
    begins = jnp.zeros((1, HEAD_DIM), jnp.int32)
    ends = jnp.full((1, HEAD_DIM), n_row * n_col * shard, jnp.int32)
    end = jnp.int32(0)
    docs = lens_ref.shape[0]
    for doc in range(docs):
        begins = jnp.where(lanes_of == doc, end, begins)
        end = end + lens_ref[doc]
        ends = jnp.where(lanes_of == doc, end, ends)
    offsets = lax.broadcasted_iota(jnp.int32, (shard, HEAD_DIM), 0)
    member = within(first + offsets) & (lanes_of < docs)
    member_ref[...] = jnp.where(member, 1.0, 0.0).astype(jnp.bfloat16)
    load_q.wait()

    def attend(blocks, fresh):
        count = shard * len(blocks)
        keys = jnp.concatenate([kv[at, which, :shard, :] for at, which in blocks], axis=0)
        vals = jnp.concatenate([kv[at, which, shard:, :] for at, which in blocks], axis=0)
        places = [at * tile + which * shard + offsets for at, which in blocks]
        apart = [jnp.where(within(place), 0.0, MASKED).astype(jnp.bfloat16) for place in places]
        kwide = jnp.concatenate([keys, jnp.concatenate(apart, axis=0)], axis=1)
        if fresh:
            kpos = first + lax.broadcasted_iota(jnp.int32, (count, shard), 0)
            bias = jnp.where(kpos <= qpos, jnp.float32(0.0), jnp.float32(MASKED))
        vflip = jnp.concatenate([vals.T, jnp.ones((SUM_ROWS, count), vals.dtype)], axis=0)

        def score(head):
            q = q_ref[:, head * HEAD_DIM : (head + 1) * HEAD_DIM]
            qwide = jnp.concatenate([q, member_ref[...]], axis=1)
            scores = lax.dot_general(
                kwide, qwide, (((1,), (1,)), ((), ())), preferred_element_type=jnp.float32
            )
            if fresh:
                scores = scores + bias
            s_ref[head % AHEAD_SLOTS, :count, :] = scores
            top = jnp.max(scores, axis=0, keepdims=True)
            if fresh:
                return top, top
            before = top_ref[head : head + 1, :]
            return before, jnp.maximum(before, top)

        tops = [score(head) for head in range(AHEAD_SLOTS - 1)]
        for head in range(heads):
            before, top = tops[head]
            if head + AHEAD_SLOTS - 1 < heads:
                tops.append(score(head + AHEAD_SLOTS - 1))
            weights = jnp.exp2((s_ref[head % AHEAD_SLOTS, :count, :] - top) * RATE)
            both = jnp.dot(vflip, weights.astype(jnp.bfloat16), preferred_element_type=jnp.float32)
            summed, total = both[:HEAD_DIM, :], both[HEAD_DIM : HEAD_DIM + 1, :]
            if not fresh:
                factor = jnp.exp2((before - top) * RATE)
                total = total + total_ref[head : head + 1, :] * factor
                summed = summed + acc_ref[head] * factor
            top_ref[head : head + 1, :] = top
            total_ref[head : head + 1, :] = total
            acc_ref[head] = summed

    attend([(row, col)], True)

    @pl.when(col > 0)
    def _():
        wait_whole(row, mate_sem.at[0])
        attend([(row, mate)], False)

    def relay(dist):
        near = straight(dist)

        @pl.when(needs(row, near))
        def _():
            up = has_up & needs(row + lanes, near)
            across = needs(other, near)
            for p in range(PIECES):
                wait_part(near, p, in_sem.at[2 * dist, p])

                @pl.when(up)
                def _():
                    to_up(near, p, dist).start()

                if has_other:

                    @pl.when(across)
                    def _():
                        to_other(near, p, dist).start()

            to_mate(near, 2 * dist).start()

        if has_other:
            far = crossed(dist - 1)

            @pl.when(needs(row, far))
            def _():
                for p in range(PIECES):
                    wait_part(far, p, in_sem.at[2 * dist - 1, p])
                to_mate(far, 2 * dist - 1).start()

    def drain(dist):
        near = straight(dist)

        @pl.when(needs(row, near))
        def _():
            @pl.when(has_up & needs(row + lanes, near))
            def _():
                wait_whole(near, up_send.at[dist])

            if has_other:

                @pl.when(needs(other, near))
                def _():
                    wait_whole(near, cross_send.at[dist])

            wait_whole(near, mate_send.at[2 * dist])

        if has_other:
            far = crossed(dist - 1)

            @pl.when(needs(row, far))
            def _():
                wait_whole(far, mate_send.at[2 * dist - 1])

    @pl.loop(1, furthest + 2)
    def _(dist):
        near, far = straight(dist), crossed(dist - 1)
        has_near = needs(row, near)
        has_far = needs(row, far) if has_other else jnp.bool_(False)
        both = has_near & has_far
        relay(dist)

        @pl.loop(0, 2)
        def _(half):
            waits = jnp.where(both, half == 1, half == 0)

            @pl.when(waits & has_near)
            def _():
                wait_whole(near, mate_sem.at[2 * dist])

            if has_other:

                @pl.when(waits & has_far)
                def _():
                    wait_whole(far, mate_sem.at[2 * dist - 1])

            @pl.when(both | ((half == 0) & (has_near | has_far)))
            def _():
                first_at = jnp.where(has_near, near, far)
                second_at = jnp.where(has_far, far, near)
                first_col = jnp.where(half == 0, col, mate)
                second_col = jnp.where(both & (half == 0), col, mate)
                attend([(first_at, first_col), (second_at, second_col)], False)

        drain(dist)

    for head in range(heads):
        inverse = 1.0 / total_ref[head : head + 1, :]
        result = (acc_ref[head] * inverse).T
        o_ref[:, head * HEAD_DIM : (head + 1) * HEAD_DIM] = result.astype(o_ref.dtype)

    @pl.when(own_up)
    def _():
        wait_whole(row, up_send.at[0])

    if has_other:

        @pl.when(own_cross)
        def _():
            wait_whole(row, cross_send.at[0])

    @pl.when(own_mate)
    def _():
        wait_whole(row, mate_send.at[0])


def shards(n_row, n_col, queries, keys, values, doc_lengths):
    shard, width = queries.shape
    lanes = 2 if n_row % 2 == 0 else 1
    span = shard * n_row * n_col
    longest = (3 * span) // 4
    reach = min(n_row - 1, -(-longest // (shard * n_col)))
    levels = n_row // lanes
    furthest = min(levels - 1, (reach + lanes - 1) // lanes)
    heads = width // HEAD_DIM
    vmem = pl.BlockSpec(memory_space=pltpu.VMEM)
    whole = pl.BlockSpec(memory_space=pltpu.HBM)
    units = 2 * furthest + 3
    return pl.pallas_call(
        functools.partial(kernel, n_row, n_col, lanes, reach),
        out_shape=jax.ShapeDtypeStruct(queries.shape, queries.dtype),
        in_specs=[pl.BlockSpec(memory_space=pltpu.SMEM), whole, whole, whole],
        out_specs=vmem,
        scratch_shapes=[
            pltpu.VMEM((n_row, n_col, 2 * shard, HEAD_DIM), keys.dtype),
            pltpu.VMEM((shard, width), queries.dtype),
            pltpu.VMEM((shard, HEAD_DIM), queries.dtype),
            pltpu.VMEM((heads, shard), jnp.float32),
            pltpu.VMEM((heads, shard), jnp.float32),
            pltpu.VMEM((heads, HEAD_DIM, shard), jnp.float32),
            pltpu.VMEM((AHEAD_SLOTS, n_col * shard, shard), jnp.float32),
            pltpu.SemaphoreType.DMA((3,)),
            pltpu.SemaphoreType.DMA((units, PIECES)),
            pltpu.SemaphoreType.DMA((units,)),
            pltpu.SemaphoreType.DMA((furthest + 2,)),
            pltpu.SemaphoreType.DMA((furthest + 2,)),
            pltpu.SemaphoreType.DMA((units,)),
        ],
        compiler_params=pltpu.CompilerParams(
            collective_id=0, has_side_effects=True, vmem_limit_bytes=24 << 20
        ),
        name="attend",
    )(*(pltpu.with_memory_space_constraint(x, pltpu.HBM) for x in (doc_lengths, queries, keys, values)))


def solution(mesh):
    placed = P(("groups", "row", "col"), None)
    return jax.shard_map(
        functools.partial(shards, mesh.shape["row"], mesh.shape["col"]),
        mesh=mesh,
        in_specs=(placed, placed, placed, P("groups")),
        out_specs=placed,
        check_vma=False,
    )
```

time: 24.1 us -> 21.7 us (0.900)
  Pallas kernels: 23.2 us -> 20.7 us
    pallas_call x1, Pallas kernels: 23.2 us -> 20.7 us  [shards(): pl.pallas_call(functools.partial(kernel, n_row, n_col, lanes, reach), out...]
where the time goes in v1:
time: 21.7 us; the launch traced here: 21.5 us
  Pallas kernels  20.7 us (95%)
  local copies, waits for them, and re-layouts  0.8 us (4%)
    pallas_call x1, Pallas kernels, shards(): pl.pallas_call(functools.partial(kernel, n_row, n_col, lanes, reach), out...  20.7 us
    unnamed x1, local copies, waits for them, and re-layouts  0.8 us

profile of v1, /device:TPU:25, one launch (start us, length us, event | category | flops | bytes accessed | tf_op | source)
XLA Modules:
  0.0 21.5 jit_solution(10876079385525908643)
XLA Ops:
  0.0 20.7 %attend.1 = bf16[256,1024]{1,0:T(8,128)(2,1)S(1)} custom-call(s32[16]{0:T(128)} %lens_ref.1, bf16[256,1024]{1,0:T(8,128)(2,1)} %q_hbm.1, bf16[256,128]{1,0:T(8,128)(2,1)} %k_hbm.1, bf16[256,128]{1,0:T(8,128)(2,1)} %v_hbm.1), custom_call_target="tpu_custom_call" | custom-call | tf_op jit(solution)/shard_map/attend/pallas_call | solution.py:334
  20.7 0.8 %copy.6 = bf16[256,1024]{1,0:T(8,128)(2,1)} copy(bf16[256,1024]{1,0:T(8,128)(2,1)S(1)} %attend.1) | data formatting | bytes 1048576

commit v2 on v1

--- a/solution.py
+++ b/solution.py
@@ -20,11 +20,12 @@
     n_col,
     lanes,
     reach,
-    lens_ref,
+    lens_hbm,
     q_hbm,
     k_hbm,
     v_hbm,
     o_ref,
+    lens_ref,
     kv,
     q_ref,
     member_ref,
@@ -80,7 +81,8 @@
     load_k = pltpu.make_async_copy(k_hbm, kv.at[row, col, :shard, :], load_sem.at[0])
     load_v = pltpu.make_async_copy(v_hbm, kv.at[row, col, shard:, :], load_sem.at[1])
     load_q = pltpu.make_async_copy(q_hbm, q_ref, load_sem.at[2])
-    for load in (load_k, load_v, load_q):
+    load_lens = pltpu.make_async_copy(lens_hbm, lens_ref, load_sem.at[3])
+    for load in (load_k, load_v, load_q, load_lens):
         load.start()
 
     def copy(source, rows, send_sem, recv_sem, device):
@@ -105,9 +107,8 @@
         recv = in_sem.at[2 * dist + 1, p]
         return copy(source, part(p), cross_send.at[dist], recv, {"row": other})
 
-    def to_mate(source, unit):
-        whole = pl.ds(0, 2 * shard)
-        return copy(source, whole, mate_send.at[unit], mate_sem.at[unit], {"col": mate})
+    def to_mate(source, p, unit):
+        return copy(source, part(p), mate_send.at[unit], mate_sem.at[unit], {"col": mate})
 
     def wait_whole(source, sem):
         here = kv.at[source, col, :, :]
@@ -140,7 +141,8 @@
 
     @pl.when(own_mate)
     def _():
-        to_mate(row, 0).start()
+        for p in range(PIECES):
+            to_mate(row, p, 0).start()
 
     first = (row * n_col + col) * shard
     qpos = first + lax.broadcasted_iota(jnp.int32, (1, shard), 1)
@@ -152,6 +154,7 @@
     begins = jnp.zeros((1, HEAD_DIM), jnp.int32)
     ends = jnp.full((1, HEAD_DIM), n_row * n_col * shard, jnp.int32)
     end = jnp.int32(0)
+    load_lens.wait()
     docs = lens_ref.shape[0]
     for doc in range(docs):
         begins = jnp.where(lanes_of == doc, end, begins)
@@ -232,7 +235,7 @@
                     def _():
                         to_other(near, p, dist).start()
 
-            to_mate(near, 2 * dist).start()
+                to_mate(near, p, 2 * dist).start()
 
         if has_other:
             far = crossed(dist - 1)
@@ -241,7 +244,22 @@
             def _():
                 for p in range(PIECES):
                     wait_part(far, p, in_sem.at[2 * dist - 1, p])
-                to_mate(far, 2 * dist - 1).start()
+                    to_mate(far, p, 2 * dist - 1).start()
+
+    def drain_own():
+        @pl.when(own_up)
+        def _():
+            wait_whole(row, up_send.at[0])
+
+        if has_other:
+
+            @pl.when(own_cross)
+            def _():
+                wait_whole(row, cross_send.at[0])
+
+        @pl.when(own_mate)
+        def _():
+            wait_whole(row, mate_send.at[0])
 
     def drain(dist):
         near = straight(dist)
@@ -275,48 +293,46 @@
         both = has_near & has_far
         relay(dist)
 
+        @pl.when(dist == 2)
+        def _():
+            drain_own()
+
+        @pl.when(dist > 1)
+        def _():
+            drain(dist - 1)
+
+        single = jnp.where(has_near, near, far)
+        single_unit = jnp.where(has_near, 2 * dist, 2 * dist - 1)
+        alone = has_near != has_far
+
         @pl.loop(0, 2)
         def _(half):
-            waits = jnp.where(both, half == 1, half == 0)
-
-            @pl.when(waits & has_near)
-            def _():
-                wait_whole(near, mate_sem.at[2 * dist])
-
-            if has_other:
-
-                @pl.when(waits & has_far)
+            which = jnp.where(half == 0, col, mate)
+
+            @pl.when(both)
+            def _():
+                @pl.when(half == 1)
                 def _():
-                    wait_whole(far, mate_sem.at[2 * dist - 1])
-
-            @pl.when(both | ((half == 0) & (has_near | has_far)))
-            def _():
-                first_at = jnp.where(has_near, near, far)
-                second_at = jnp.where(has_far, far, near)
-                first_col = jnp.where(half == 0, col, mate)
-                second_col = jnp.where(both & (half == 0), col, mate)
-                attend([(first_at, first_col), (second_at, second_col)], False)
-
-        drain(dist)
+                    wait_whole(near, mate_sem.at[2 * dist])
+                    if has_other:
+                        wait_whole(far, mate_sem.at[2 * dist - 1])
+
+                attend([(near, which), (far, which)], False)
+
+            @pl.when(alone)
+            def _():
+                @pl.when(half == 1)
+                def _():
+                    wait_whole(single, mate_sem.at[single_unit])
+
+                attend([(single, which)], False)
 
     for head in range(heads):
         inverse = 1.0 / total_ref[head : head + 1, :]
         result = (acc_ref[head] * inverse).T
         o_ref[:, head * HEAD_DIM : (head + 1) * HEAD_DIM] = result.astype(o_ref.dtype)
 
-    @pl.when(own_up)
-    def _():
-        wait_whole(row, up_send.at[0])
-
-    if has_other:
-
-        @pl.when(own_cross)
-        def _():
-            wait_whole(row, cross_send.at[0])
-
-    @pl.when(own_mate)
-    def _():
-        wait_whole(row, mate_send.at[0])
+    drain(furthest + 1)
 
 
 def shards(n_row, n_col, queries, keys, values, doc_lengths):
@@ -334,9 +350,10 @@
     return pl.pallas_call(
         functools.partial(kernel, n_row, n_col, lanes, reach),
         out_shape=jax.ShapeDtypeStruct(queries.shape, queries.dtype),
-        in_specs=[pl.BlockSpec(memory_space=pltpu.SMEM), whole, whole, whole],
+        in_specs=[whole, whole, whole, whole],
         out_specs=vmem,
         scratch_shapes=[
+            pltpu.SMEM(doc_lengths.shape, doc_lengths.dtype),
             pltpu.VMEM((n_row, n_col, 2 * shard, HEAD_DIM), keys.dtype),
             pltpu.VMEM((shard, width), queries.dtype),
             pltpu.VMEM((shard, HEAD_DIM), queries.dtype),
@@ -344,7 +361,7 @@
             pltpu.VMEM((heads, shard), jnp.float32),
             pltpu.VMEM((heads, HEAD_DIM, shard), jnp.float32),
             pltpu.VMEM((AHEAD_SLOTS, n_col * shard, shard), jnp.float32),
-            pltpu.SemaphoreType.DMA((3,)),
+            pltpu.SemaphoreType.DMA((4,)),
             pltpu.SemaphoreType.DMA((units, PIECES)),
             pltpu.SemaphoreType.DMA((units,)),
             pltpu.SemaphoreType.DMA((furthest + 2,)),

time: 21.7 us -> 20.2 us (0.931)
  Pallas kernels: 20.7 us -> 19.2 us
    pallas_call x1, Pallas kernels: 20.7 us -> 19.2 us  [shards(): pl.pallas_call(functools.partial(kernel, n_row, n_col, lanes, reach), out...]
where the time goes in v2:
time: 20.2 us; the launch traced here: 20 us
  Pallas kernels  19.2 us (95%)
  local copies, waits for them, and re-layouts  0.8 us (4%)
    pallas_call x1, Pallas kernels, shards(): pl.pallas_call(functools.partial(kernel, n_row, n_col, lanes, reach), out...  19.2 us
    unnamed x1, local copies, waits for them, and re-layouts  0.8 us

profile of v2, /device:TPU:25, one launch (start us, length us, event | category | flops | bytes accessed | tf_op | source)
XLA Modules:
  0.0 20.0 jit_solution(3931166649110940460)
XLA Ops:
  0.0 19.2 %attend.1 = bf16[256,1024]{1,0:T(8,128)(2,1)S(1)} custom-call(s32[16]{0:T(128)} %lens_hbm.1, bf16[256,1024]{1,0:T(8,128)(2,1)} %q_hbm.1, bf16[256,128]{1,0:T(8,128)(2,1)} %k_hbm.1, bf16[256,128]{1,0:T(8,128)(2,1)} %v_hbm.1), custom_call_target="tpu_custom_call" | custom-call | tf_op jit(solution)/shard_map/attend/pallas_call | solution.py:350
  19.2 0.8 %copy.6 = bf16[256,1024]{1,0:T(8,128)(2,1)} copy(bf16[256,1024]{1,0:T(8,128)(2,1)S(1)} %attend.1) | data formatting | bytes 1048576

commit v3 on v2

--- a/solution.py
+++ b/solution.py
@@ -12,7 +12,8 @@
 MASKED = -1e30
 AHEAD_SLOTS = 8
 SUM_ROWS = 16
-PIECES = 2
+CUTS = (0, 1, 2)
+PIECES = len(CUTS) - 1
 
 
 def kernel(
@@ -39,12 +40,13 @@
     up_send,
     cross_send,
     mate_send,
+    far_send,
 ):
     shard = q_hbm.shape[0]
     heads = q_hbm.shape[1] // HEAD_DIM
     levels = n_row // lanes
     tile = n_col * shard
-    piece = 2 * shard // PIECES
+    cuts = [2 * shard * cut // CUTS[-1] for cut in CUTS]
     furthest = min(levels - 1, (reach + lanes - 1) // lanes)
     has_other = lanes > 1
     row = lax.axis_index("row")
@@ -79,9 +81,9 @@
         pl.semaphore_signal(barrier, inc=1, device_id={"row": row - lanes})
 
     load_k = pltpu.make_async_copy(k_hbm, kv.at[row, col, :shard, :], load_sem.at[0])
-    load_v = pltpu.make_async_copy(v_hbm, kv.at[row, col, shard:, :], load_sem.at[1])
-    load_q = pltpu.make_async_copy(q_hbm, q_ref, load_sem.at[2])
-    load_lens = pltpu.make_async_copy(lens_hbm, lens_ref, load_sem.at[3])
+    load_v = pltpu.make_async_copy(v_hbm, kv.at[row, col, shard:, :], load_sem.at[0])
+    load_q = pltpu.make_async_copy(q_hbm, q_ref, load_sem.at[1])
+    load_lens = pltpu.make_async_copy(lens_hbm, lens_ref, load_sem.at[2])
     for load in (load_k, load_v, load_q, load_lens):
         load.start()
 
@@ -97,18 +99,36 @@
         )
 
     def part(p):
-        return pl.ds(p * piece, piece)
+        return pl.ds(cuts[p], cuts[p + 1] - cuts[p])
 
     def to_up(source, p, dist):
+        recv = in_sem.at[2 * dist + 1, p]
+        return copy(source, part(p), up_send.at[dist % 2], recv, {"row": row + lanes})
+
+    def to_other(source, p, dist):
+        recv = in_sem.at[2 * dist, p]
+        return copy(source, part(p), cross_send.at[dist % 2], recv, {"row": other})
+
+    split_level = levels - 3
+    late_from = PIECES // 2
+    splits = has_other and split_level >= 0
+
+    def split(source):
+        return source == split_level * lanes + lanes - 1
+
+    def far_up(source):
+        return split(source) & has_up & needs(row + lanes, source)
+
+    def to_far_up(source, p, dist):
         recv = in_sem.at[2 * dist + 2, p]
-        return copy(source, part(p), up_send.at[dist], recv, {"row": row + lanes})
-
-    def to_other(source, p, dist):
-        recv = in_sem.at[2 * dist + 1, p]
-        return copy(source, part(p), cross_send.at[dist], recv, {"row": other})
+        return copy(source, part(p), far_send.at[0], recv, {"row": row + lanes})
+
+    def wait_rows(source, start, stop, sem):
+        here = kv.at[source, col, start:stop, :]
+        pltpu.make_async_copy(here, here, sem).wait()
 
     def to_mate(source, p, unit):
-        return copy(source, part(p), mate_send.at[unit], mate_sem.at[unit], {"col": mate})
+        return copy(source, part(p), mate_send.at[unit % 4], mate_sem.at[unit], {"col": mate})
 
     def wait_whole(source, sem):
         here = kv.at[source, col, :, :]
@@ -124,8 +144,7 @@
 
     count = 1 + int(has_other) + has_up.astype(jnp.int32) + has_down.astype(jnp.int32)
     pl.semaphore_wait(barrier, count)
-    load_k.wait()
-    load_v.wait()
+    wait_whole(row, load_sem.at[0])
 
     @pl.when(own_up)
     def _():
@@ -137,6 +156,13 @@
         @pl.when(own_cross)
         def _():
             for p in range(PIECES):
+                to_other(row, p, 0).start()
+
+    if splits:
+
+        @pl.when(split(row) & has_up)
+        def _():
+            for p in range(late_from, PIECES):
                 to_other(row, p, 0).start()
 
     @pl.when(own_mate)
@@ -215,15 +241,16 @@
         wait_whole(row, mate_sem.at[0])
         attend([(row, mate)], False)
 
-    def relay(dist):
+    def relay_near(dist):
         near = straight(dist)
 
         @pl.when(needs(row, near))
         def _():
             up = has_up & needs(row + lanes, near)
             across = needs(other, near)
+            across_late = across & jnp.logical_not(split(near)) if splits else across
             for p in range(PIECES):
-                wait_part(near, p, in_sem.at[2 * dist, p])
+                wait_part(near, p, in_sem.at[2 * dist - 1, p])
 
                 @pl.when(up)
                 def _():
@@ -231,59 +258,94 @@
 
                 if has_other:
 
-                    @pl.when(across)
+                    @pl.when(across_late if p >= late_from else across)
                     def _():
                         to_other(near, p, dist).start()
 
                 to_mate(near, p, 2 * dist).start()
 
+    def relay_far(dist):
+        far = crossed(dist)
+
+        @pl.when(needs(row, far))
+        def _():
+            for p in range(PIECES):
+                wait_part(far, p, in_sem.at[2 * dist, p])
+                if splits and p >= late_from:
+
+                    @pl.when(far_up(far))
+                    def _():
+                        to_far_up(far, p, dist).start()
+
+                to_mate(far, p, 2 * dist + 1).start()
+
+        if splits:
+
+            @pl.when((far > row) & far_up(far))
+            def _():
+                for p in range(late_from, PIECES):
+                    wait_part(far, p, in_sem.at[2 * dist, p])
+                    to_far_up(far, p, dist).start()
+
+    def early(dist):
+        return (lane == lanes - 1) & (level == dist + 1) & (dist >= 1)
+
+    def drain_own():
+        @pl.when(own_up)
+        def _():
+            wait_whole(row, up_send.at[0])
+
+        if has_other:
+
+            @pl.when(own_cross)
+            def _():
+                wait_whole(row, cross_send.at[0])
+
+        if splits:
+
+            @pl.when(split(row) & has_up)
+            def _():
+                wait_rows(row, cuts[late_from], cuts[-1], cross_send.at[0])
+
+        @pl.when(own_mate)
+        def _():
+            wait_whole(row, mate_send.at[0])
+
+    def drain(dist):
+        near = straight(dist)
+
+        @pl.when(needs(row, near))
+        def _():
+            @pl.when(has_up & needs(row + lanes, near))
+            def _():
+                wait_whole(near, up_send.at[dist % 2])
+
+            if has_other:
+
+                if splits:
+
+                    @pl.when(needs(other, near) & split(near))
+                    def _():
+                        wait_rows(near, 0, cuts[late_from], cross_send.at[dist % 2])
+
+                @pl.when(needs(other, near) & jnp.logical_not(split(near)) if splits else needs(other, near))
+                def _():
+                    wait_whole(near, cross_send.at[dist % 2])
+
+            wait_whole(near, mate_send.at[2 * dist % 4])
+
         if has_other:
             far = crossed(dist - 1)
 
             @pl.when(needs(row, far))
             def _():
-                for p in range(PIECES):
-                    wait_part(far, p, in_sem.at[2 * dist - 1, p])
-                    to_mate(far, p, 2 * dist - 1).start()
-
-    def drain_own():
-        @pl.when(own_up)
-        def _():
-            wait_whole(row, up_send.at[0])
-
-        if has_other:
-
-            @pl.when(own_cross)
-            def _():
-                wait_whole(row, cross_send.at[0])
-
-        @pl.when(own_mate)
-        def _():
-            wait_whole(row, mate_send.at[0])
-
-    def drain(dist):
-        near = straight(dist)
-
-        @pl.when(needs(row, near))
-        def _():
-            @pl.when(has_up & needs(row + lanes, near))
-            def _():
-                wait_whole(near, up_send.at[dist])
-
-            if has_other:
-
-                @pl.when(needs(other, near))
+                wait_whole(far, mate_send.at[(2 * dist - 1) % 4])
+
+            if splits:
+
+                @pl.when(far_up(far))
                 def _():
-                    wait_whole(near, cross_send.at[dist])
-
-            wait_whole(near, mate_send.at[2 * dist])
-
-        if has_other:
-            far = crossed(dist - 1)
-
-            @pl.when(needs(row, far))
-            def _():
-                wait_whole(far, mate_send.at[2 * dist - 1])
+                    wait_rows(far, cuts[late_from], cuts[-1], far_send.at[0])
 
     @pl.loop(1, furthest + 2)
     def _(dist):
@@ -291,9 +353,14 @@
         has_near = needs(row, near)
         has_far = needs(row, far) if has_other else jnp.bool_(False)
         both = has_near & has_far
-        relay(dist)
-
-        @pl.when(dist == 2)
+        @pl.when(jnp.logical_not(early(dist - 1)))
+        def _():
+            relay_near(dist)
+
+        if has_other:
+            relay_far(dist - 1)
+
+        @pl.when(dist == 1)
         def _():
             drain_own()
 
@@ -318,6 +385,10 @@
                         wait_whole(far, mate_sem.at[2 * dist - 1])
 
                 attend([(near, which), (far, which)], False)
+
+            @pl.when((half == 0) & early(dist))
+            def _():
+                relay_near(dist + 1)
 
             @pl.when(alone)
             def _():
@@ -346,7 +417,7 @@
     heads = width // HEAD_DIM
     vmem = pl.BlockSpec(memory_space=pltpu.VMEM)
     whole = pl.BlockSpec(memory_space=pltpu.HBM)
-    units = 2 * furthest + 3
+    units = 2 * furthest + 2
     return pl.pallas_call(
         functools.partial(kernel, n_row, n_col, lanes, reach),
         out_shape=jax.ShapeDtypeStruct(queries.shape, queries.dtype),
@@ -361,12 +432,13 @@
             pltpu.VMEM((heads, shard), jnp.float32),
             pltpu.VMEM((heads, HEAD_DIM, shard), jnp.float32),
             pltpu.VMEM((AHEAD_SLOTS, n_col * shard, shard), jnp.float32),
+            pltpu.SemaphoreType.DMA((3,)),
+            pltpu.SemaphoreType.DMA((units - 1, PIECES)),
+            pltpu.SemaphoreType.DMA((units,)),
+            pltpu.SemaphoreType.DMA((2,)),
+            pltpu.SemaphoreType.DMA((2,)),
             pltpu.SemaphoreType.DMA((4,)),
-            pltpu.SemaphoreType.DMA((units, PIECES)),
-            pltpu.SemaphoreType.DMA((units,)),
-            pltpu.SemaphoreType.DMA((furthest + 2,)),
-            pltpu.SemaphoreType.DMA((furthest + 2,)),
-            pltpu.SemaphoreType.DMA((units,)),
+            pltpu.SemaphoreType.DMA((1,)),
         ],
         compiler_params=pltpu.CompilerParams(
             collective_id=0, has_side_effects=True, vmem_limit_bytes=24 << 20

time: 20.2 us -> 19.7 us (0.975)
  Pallas kernels: 19.2 us -> 18.7 us
    pallas_call x1, Pallas kernels: 19.2 us -> 18.7 us  [shards(): pl.pallas_call(functools.partial(kernel, n_row, n_col, lanes, reach), out...]
where the time goes in v3:
time: 19.7 us; the launch traced here: 19.5 us
  Pallas kernels  18.7 us (95%)
  local copies, waits for them, and re-layouts  0.8 us (4%)
    pallas_call x1, Pallas kernels, shards(): pl.pallas_call(functools.partial(kernel, n_row, n_col, lanes, reach), out...  18.7 us
    unnamed x1, local copies, waits for them, and re-layouts  0.8 us

profile of v3, /device:TPU:25, one launch (start us, length us, event | category | flops | bytes accessed | tf_op | source)
XLA Modules:
  0.0 19.5 jit_solution(10556562843326773554)
XLA Ops:
  0.0 18.7 %attend.1 = bf16[256,1024]{1,0:T(8,128)(2,1)S(1)} custom-call(s32[16]{0:T(128)} %lens_hbm.1, bf16[256,1024]{1,0:T(8,128)(2,1)} %q_hbm.1, bf16[256,128]{1,0:T(8,128)(2,1)} %k_hbm.1, bf16[256,128]{1,0:T(8,128)(2,1)} %v_hbm.1), custom_call_target="tpu_custom_call" | custom-call | tf_op jit(solution)/shard_map/attend/pallas_call | solution.py:421
  18.7 0.8 %copy.6 = bf16[256,1024]{1,0:T(8,128)(2,1)} copy(bf16[256,1024]{1,0:T(8,128)(2,1)S(1)} %attend.1) | data formatting | bytes 1048576

commit v4 on v3

--- a/solution.py
+++ b/solution.py
@@ -10,7 +10,7 @@
 HEAD_DIM = 128
 RATE = HEAD_DIM ** (-0.5) * 1.4426950408889634
 MASKED = -1e30
-AHEAD_SLOTS = 8
+AHEAD_SLOTS = 7
 SUM_ROWS = 16
 CUTS = (0, 1, 2)
 PIECES = len(CUTS) - 1

time: 19.7 us -> 19.4 us (0.985)
  Pallas kernels: 18.7 us -> 18.5 us
    pallas_call x1, Pallas kernels: 18.7 us -> 18.5 us  [shards(): pl.pallas_call(functools.partial(kernel, n_row, n_col, lanes, reach), out...]
where the time goes in v4:
time: 19.4 us; the launch traced here: 19.3 us
  Pallas kernels  18.5 us (95%)
  local copies, waits for them, and re-layouts  0.8 us (4%)
    pallas_call x1, Pallas kernels, shards(): pl.pallas_call(functools.partial(kernel, n_row, n_col, lanes, reach), out...  18.5 us
    unnamed x1, local copies, waits for them, and re-layouts  0.8 us

profile of v4, /device:TPU:25, one launch (start us, length us, event | category | flops | bytes accessed | tf_op | source)
XLA Modules:
  0.0 19.3 jit_solution(4487231022829950917)
XLA Ops:
  0.0 18.5 %attend.1 = bf16[256,1024]{1,0:T(8,128)(2,1)S(1)} custom-call(s32[16]{0:T(128)} %lens_hbm.1, bf16[256,1024]{1,0:T(8,128)(2,1)} %q_hbm.1, bf16[256,128]{1,0:T(8,128)(2,1)} %k_hbm.1, bf16[256,128]{1,0:T(8,128)(2,1)} %v_hbm.1), custom_call_target="tpu_custom_call" | custom-call | tf_op jit(solution)/shard_map/attend/pallas_call | solution.py:421
  18.5 0.8 %copy.6 = bf16[256,1024]{1,0:T(8,128)(2,1)} copy(bf16[256,1024]{1,0:T(8,128)(2,1)S(1)} %attend.1) | data formatting | bytes 1048576

commit v5 on v4

--- a/solution.py
+++ b/solution.py
@@ -12,7 +12,7 @@
 MASKED = -1e30
 AHEAD_SLOTS = 7
 SUM_ROWS = 16
-CUTS = (0, 1, 2)
+CUTS = (0, 5, 8)
 PIECES = len(CUTS) - 1
 
 

time: 19.4 us -> 19 us (0.979)
  Pallas kernels: 18.5 us -> 18.1 us
    pallas_call x1, Pallas kernels: 18.5 us -> 18.1 us  [shards(): pl.pallas_call(functools.partial(kernel, n_row, n_col, lanes, reach), out...]
where the time goes in v5:
time: 19 us; the launch traced here: 18.9 us
  Pallas kernels  18.1 us (95%)
  local copies, waits for them, and re-layouts  0.8 us (4%)
    pallas_call x1, Pallas kernels, shards(): pl.pallas_call(functools.partial(kernel, n_row, n_col, lanes, reach), out...  18.1 us
    unnamed x1, local copies, waits for them, and re-layouts  0.8 us

profile of v5, /device:TPU:25, one launch (start us, length us, event | category | flops | bytes accessed | tf_op | source)
XLA Modules:
  0.0 18.9 jit_solution(14200606553524051048)
XLA Ops:
  0.0 18.1 %attend.1 = bf16[256,1024]{1,0:T(8,128)(2,1)S(1)} custom-call(s32[16]{0:T(128)} %lens_hbm.1, bf16[256,1024]{1,0:T(8,128)(2,1)} %q_hbm.1, bf16[256,128]{1,0:T(8,128)(2,1)} %k_hbm.1, bf16[256,128]{1,0:T(8,128)(2,1)} %v_hbm.1), custom_call_target="tpu_custom_call" | custom-call | tf_op jit(solution)/shard_map/attend/pallas_call | solution.py:421
  18.1 0.8 %copy.6 = bf16[256,1024]{1,0:T(8,128)(2,1)} copy(bf16[256,1024]{1,0:T(8,128)(2,1)S(1)} %attend.1) | data formatting | bytes 1048576
